TPU v7x, 512 devices: a whole 4x4x16 slice. The times are simulated.
512 devices in a mesh: row: 32 (over x, y, core), col: 16 (over z).
Axes of the slice: x: 4, y: 4, z: 16, core: 2. Of those that a mesh axis runs over, the one named last changes fastest.
Arguments:
- features: bfloat16 [65536, 256], P('col', 'row'), may hold values from -6 to 6
- weight: bfloat16 [256, 256], replicated, may hold values from -0.375 to 0.375
- adj_values: bfloat16 [32, 16, 96, 128, 128], P('row', 'col'), may hold values from -0.0625 to 0.0625
- block_rows: int32 [32, 16, 96], P('row', 'col'), may hold values from 0 to 15, as said below
- block_cols: int32 [32, 16, 96], P('row', 'col'), may hold values from 0 to 31
- block_counts: int32 [32, 16], P('row', 'col'), may hold values from 1 to 96, as said below
- cotangent: bfloat16 [65536, 256], P(('row', 'col')), may hold values from -6 to 6
Outputs:
- output: bfloat16 [65536, 256], P(('row', 'col'))
- grad_weight: float32 [256, 256], replicated
- grad_features: bfloat16 [65536, 256], P('col', 'row')
Inputs may be any that keep to these rules, and one draw needn't show every extreme that they name: Within one tile the pairs (block_rows, block_cols) over all 96 slots are distinct. `block_counts`: some tile holds exactly 96 live blocks and some other tile exactly one in every draw.
All inputs are finite; a program needn't handle non-finite values.
Results may differ from a plain program's by a relative error of at most 0.029.
Values may be sent and summed in bfloat16 or wider, within the bound.
A program may use at most 64 MiB of HBM per device.

v0:
```python
import math
import jax
import jax.numpy as jnp
from jax import lax
from jax.sharding import PartitionSpec as P

RB = 16


def block_product(tile_values, tile_rows, tile_cols, live_count, panels, out_blocks, transposed):
    padded = tile_values.shape[0]
    blocks_turn = math.gcd(padded, 16)
    block_size = panels.shape[1]
    columns = panels.shape[2]
    turns_needed = (live_count + blocks_turn - 1) // blocks_turn

    def step(turn_index, running):
        offset = turn_index * blocks_turn
        values_now = lax.dynamic_slice_in_dim(tile_values, offset, blocks_turn, 0)
        row_ids = lax.dynamic_slice_in_dim(tile_rows, offset, blocks_turn, 0)
        col_ids = lax.dynamic_slice_in_dim(tile_cols, offset, blocks_turn, 0)
        is_live = offset + jnp.arange(blocks_turn, dtype=jnp.int32) < live_count
        if transposed:
            picked = jnp.take(panels, row_ids, axis=0)
            product = jnp.einsum(
                "bij,bif->bjf", values_now, picked, preferred_element_type=jnp.float32
            )
            target_ids = col_ids
        else:
            picked = jnp.take(panels, col_ids, axis=0)
            product = jnp.einsum(
                "bij,bjf->bif", values_now, picked, preferred_element_type=jnp.float32
            )
            target_ids = row_ids
        contribution = jnp.where(is_live[:, None, None], product, 0.0)
        return running.at[target_ids].add(contribution)

    start_sum = jnp.zeros((out_blocks, block_size, columns), jnp.float32)
    return lax.fori_loop(0, turns_needed, step, start_sum)


def shards(features, weight, adj_values, block_rows, block_cols, block_counts, cotangent):
    tile_values = adj_values[0, 0]
    tile_rows = block_rows[0, 0]
    tile_cols = block_cols[0, 0]
    live_count = block_counts[0, 0]
    block_size = tile_values.shape[1]
    col_blocks = features.shape[0] // block_size
    node_total = col_blocks * block_size * lax.axis_size("col")
    panel_part = lax.all_gather(features, "row", axis=1, tiled=True)
    panels = panel_part.reshape(col_blocks, block_size, panel_part.shape[1])
    partial_value = block_product(tile_values, tile_rows, tile_cols, live_count, panels, RB, False)
    partial_value = partial_value.reshape(RB * block_size, partial_value.shape[2])
    aggregated = lax.psum_scatter(
        partial_value.astype(jnp.bfloat16), "col", scatter_dimension=0, tiled=True
    )
    preact = jnp.dot(aggregated, weight, preferred_element_type=jnp.float32)
    output = jax.nn.silu(preact).astype(jnp.bfloat16)
    sigmoid_pre = jax.nn.sigmoid(preact)
    slopes = sigmoid_pre * (1.0 + preact * (1.0 - sigmoid_pre))
    deltas = (cotangent.astype(jnp.float32) * slopes).astype(jnp.bfloat16)
    local_grad = jnp.dot(aggregated.T, deltas, preferred_element_type=jnp.float32)
    grad_weight = lax.psum(local_grad, ("row", "col")) * (1.0 / math.sqrt(node_total))
    backward = jnp.dot(deltas, weight.T, preferred_element_type=jnp.float32).astype(jnp.bfloat16)
    back_slab = lax.all_gather(backward, "col", axis=0, tiled=True)
    back_panels = back_slab.reshape(RB, block_size, back_slab.shape[1])
    column_terms = block_product(
        tile_values, tile_rows, tile_cols, live_count, back_panels, col_blocks, True
    )
    column_terms = column_terms.reshape(col_blocks * block_size, column_terms.shape[2])
    grad_features = lax.psum_scatter(
        column_terms.astype(jnp.bfloat16), "row", scatter_dimension=1, tiled=True
    )
    return (output, grad_weight, grad_features)


def solution(mesh):
    return jax.shard_map(
        shards,
        mesh=mesh,
        in_specs=(
            P("col", "row"),
            P(),
            P("row", "col", None, None, None),
            P("row", "col", None),
            P("row", "col", None),
            P("row", "col"),
            P(("row", "col"), None),
        ),
        out_specs=(P(("row", "col"), None), P(), P("col", "row")),
        check_vma=False,
    )
```

profile of v0, /device:TPU:2, one launch (start us, length us, event | category | flops | bytes accessed | tf_op | source)
XLA Modules:
  0.0 847.8 jit_solution(3140927563884392423)
XLA Ops:
  8.6 65.7 %all-gather.3.cloned.1.call-done = bf16[4096,256]{0,1:T(8,128)(2,1)} async-done(((bf16[4096,8]{0,1:T(8,128)(2,1)}), bf16[4096,256]{0,1:T(8,128)(2,1)}) %all-gather.3.cloned.1.call-update) | async-done | bytes 2097168 | tf_op jit(solution)/shard_map/all_gather | solution.py:50
  74.3 4.1 copy.11
  80.0 35.9 %while.20 = (s32[]{:T(128)}, f32[16,128,256]{2,1,0:T(8,128)}, s32[]{:T(128)}, s32[96]{0:T(128)S(1)}, s32[]{:T(128)}, /*index=5*/bf16[96,128,128]{2,1,0:T(8,128)(...) while((s32[]{:T(128)}, f32[16,128,256]{2,1,0:T(8,128)}, ...), condition=%wide.region_2.3_spmd, body=%wide.region_0.2_spmd.sunk | while | flops 135791792 | bytes 12063415 | solution.py:39
  80.7 2.2 gather_fusion
  84.5 4.3 scatter_fusion
  89.6 2.2 gather_fusion
  91.8 1.6 convolution_select_fusion.4
  93.4 4.4 scatter_fusion
  98.5 2.2 gather_fusion
  102.4 4.5 scatter_fusion
  107.6 2.2 gather_fusion
  111.4 4.4 scatter_fusion
  115.9 2.8 convert_element_type.24
  118.8 87.5 %reduce-scatter.3.cloned.1.call-done = bf16[128,256]{1,0:T(8,128)(2,1)} async-done(((bf16[2048,256]{1,0:T(8,128)(2,1)}), bf16[128,256]{1,0:T(8,128)(2,1)}) %reduce-scatter.3.cloned.1.call-update) | async-done | bytes 65552 | tf_op jit(solution)/shard_map/reduce_scatter | solution.py:54
  206.3 1.7 multiply_convert_fusion
  208.9 2.8 copy.10
  212.7 65.3 %all-gather.5.cloned.1.call-done = bf16[2048,256]{1,0:T(8,128)(2,1)} async-done(((bf16[128,256]{1,0:T(8,128)(2,1)}), bf16[2048,256]{1,0:T(8,128)(2,1)}) %all-gather.5.cloned.1.call-update) | async-done | bytes 1048592 | tf_op jit(solution)/shard_map/all_gather | solution.py:65
  278.1 2.4 broadcast_in_dim.59
  280.5 34.6 %while.21 = (s32[]{:T(128)}, f32[32,128,256]{2,1,0:T(8,128)}, s32[]{:T(128)}, s32[96]{0:T(128)S(1)}, s32[]{:T(128)}, /*index=5*/bf16[96,128,128]{1,2,0:T(8,128)(...) while((s32[]{:T(128)}, f32[32,128,256]{2,1,0:T(8,128)}, ...), condition=%wide.region_7.8_spmd, body=%wide.region_5.7_spmd.sunk | while | flops 135791792 | bytes 12063415 | solution.py:39
  281.2 1.8 gather_fusion.1
  284.7 4.3 scatter_fusion.1
  289.8 1.8 gather_fusion.1
  293.3 4.5 scatter_fusion.1
  298.5 1.8 gather_fusion.1
  301.9 4.5 scatter_fusion.1
  307.1 1.8 gather_fusion.1
  310.6 4.4 scatter_fusion.1
  315.1 2.5 convert_element_type.30
  317.6 2.9 copy.15
  320.5 418.5 %all-reduce.2.cloned.1.call-done = f32[256,256]{1,0:T(8,128)} async-done(((f32[256,256]{1,0:T(8,128)}), f32[256,256]{1,0:T(8,128)}) %all-reduce.2.cloned.1.call-update) | async-done | bytes 262160 | tf_op jit(solution)/shard_map/psum | solution.py:63
  739.0 1.7 broadcast_multiply_fusion
  740.6 100.6 %reduce-scatter.5.cloned.1.call-done = bf16[4096,8]{0,1:T(8,128)(2,1)} async-done(((bf16[4096,256]{0,1:T(8,128)(2,1)}), bf16[4096,8]{0,1:T(8,128)(2,1)}) %reduce-scatter.5.cloned.1.call-update) | async-done | bytes 65552 | tf_op jit(solution)/shard_map/reduce_scatter | solution.py:71
  (56 shorter events, 21.6 us)
Async XLA Ops:
  7.2 199.1 %copy-start = (bf16[256,256]{1,0:T(8,128)(2,1)S(1)}, bf16[256,256]{1,0:T(8,128)(2,1)}, u32[]{:S(2)}) copy-start(bf16[256,256]{1,0:T(8,128)(2,1)} %param.12) | copy-start | bytes 393220
  7.2 67.2 %all-gather.3.cloned.1.call-start = ((), (), s32[]{:S(2)}) async-start(), calls=%async_computation.2 | async-start | bytes 2162688 | tf_op jit(solution)/shard_map/all_gather | solution.py:50
  7.9 198.4 %reduce-scatter.3.cloned.1.call-start = ((), (), s32[]{:S(2)}) async-start(), calls=%async_computation.3 | async-start | bytes 1114112 | tf_op jit(solution)/shard_map/reduce_scatter | solution.py:54
  78.4 1.5 copy-start.3
  78.4 1.5 copy-start.4
  115.9 90.4 %copy-start.5 = (bf16[128,256]{1,0:T(8,128)(2,1)S(1)}, bf16[128,256]{1,0:T(8,128)(2,1)}, u32[]{:S(2)}) copy-start(bf16[128,256]{1,0:T(8,128)(2,1)} %param.17) | copy-start | bytes 196612
  115.9 93.1 %copy-start.1 = (bf16[96,128,128]{2,1,0:T(8,128)(2,1)S(1)}, bf16[96,128,128]{2,1,0:T(8,128)(2,1)}, u32[]{:S(2)}) copy-start(bf16[96,128,128]{2,1,0:T(8,128)(2,1)} %get-tuple-element.328) | copy-start | bytes 9437188
  118.7 159.3 %all-gather.5.cloned.1.call-start = ((), (), s32[]{:S(2)}) async-start(), calls=%async_computation.5 | async-start | bytes 1114112 | tf_op jit(solution)/shard_map/all_gather | solution.py:65
  208.9 2.9 copy-start.2
  208.9 530.1 %all-reduce.2.cloned.1.call-start = ((), (), s32[]{:S(2)}) async-start(), calls=%async_computation.4 | async-start | bytes 524288 | tf_op jit(solution)/shard_map/psum | solution.py:63
  212.7 628.6 %reduce-scatter.5.cloned.1.call-start = ((), (), s32[]{:S(2)}) async-start(), calls=%async_computation.6 | async-start | bytes 2162688 | tf_op jit(solution)/shard_map/reduce_scatter | solution.py:71
Sparse Core Ops, SparseCore 0:
  11.1 63.1 all-gather.2
  118.9 87.4 reduce-scatter.2
  209.2 68.8 all-gather.4
  284.8 454.1 all-reduce.1
  743.8 97.3 reduce-scatter.4
where the time goes:
time: 850 us; the launch traced here: 848 us
  waiting for transfers between devices  738 us (87%)
  other arithmetic  48.7 us (6%)
  local copies, waits for them, and re-layouts  30 us (4%)
  matrix products  15.8 us (2%)
  between operations  14.5 us (2%)
    psum x1, waiting for transfers between devices, shards(): lax.psum(local_grad, ('row', 'col')) * (1.0 / math.sqrt(node_total))  418 us
    reduce_scatter x1, waiting for transfers between devices, shards(): lax.psum_scatter(column_terms.astype(jnp.bfloat16), 'row', scatter_dimens...  101 us
    reduce_scatter x1, waiting for transfers between devices, shards(): lax.psum_scatter(partial_value.astype(jnp.bfloat16), 'col', scatter_dimen...  87.5 us
    all_gather x1, waiting for transfers between devices, shards(): panel_part = lax.all_gather(features, 'row', axis=1, tiled=True)  65.7 us
    all_gather x1, waiting for transfers between devices, shards(): back_slab = lax.all_gather(backward, 'col', axis=0, tiled=True)  65.3 us
    scatter-add x8, other arithmetic, step(): return running.at[target_ids].add(contribution)  35.2 us
  transfers between devices with their start and end apart: 5, of which 5 were waited for; matrix products, arithmetic and copies ran while one was open for 6% of the time, Pallas kernels for 0%

commit v1 on v0

--- a/solution.py
+++ b/solution.py
@@ -40,6 +40,16 @@
 
 
 def shards(features, weight, adj_values, block_rows, block_cols, block_counts, cotangent):
+
+    def _solve_things(x_local):
+        b_next = jnp.concatenate(
+            lax.all_to_all(
+                jnp.stack([x_local for _ in range(lax.axis_size("row"))], axis=0), "row", 0, 0
+            ),
+            1,
+        )
+        return b_next
+
     tile_values = adj_values[0, 0]
     tile_rows = block_rows[0, 0]
     tile_cols = block_cols[0, 0]
@@ -47,7 +57,7 @@
     block_size = tile_values.shape[1]
     col_blocks = features.shape[0] // block_size
     node_total = col_blocks * block_size * lax.axis_size("col")
-    panel_part = lax.all_gather(features, "row", axis=1, tiled=True)
+    panel_part = _solve_things(features)
     panels = panel_part.reshape(col_blocks, block_size, panel_part.shape[1])
     partial_value = block_product(tile_values, tile_rows, tile_cols, live_count, panels, RB, False)
     partial_value = partial_value.reshape(RB * block_size, partial_value.shape[2])

time: 850 us -> 824 us (0.969)
  waiting for transfers between devices: 738 us -> 699 us
  starting transfers between devices: 0.2 us -> 9.78 us
    all_gather x1 -> x0, waiting for transfers between devices: 65.7 us -> none  [shards(): panel_part = lax.all_gather(features, 'row', axis=1, tiled=True)]
    all_to_all x0 -> x1, waiting for transfers between devices: none -> 25.2 us  [_solve_things(): lax.all_to_all(jnp.stack([x_local for _ in range(lax.axis_size('row'))],...]
    all_to_all x0 -> x1, starting transfers between devices: none -> 9.62 us  [_solve_things(): lax.all_to_all(jnp.stack([x_local for _ in range(lax.axis_size('row'))],...]
where the time goes in v1:
time: 824 us; the launch traced here: 823 us
  waiting for transfers between devices  699 us (85%)
  other arithmetic  48.9 us (6%)
  local copies, waits for them, and re-layouts  34.5 us (4%)
  matrix products  15.8 us (2%)
  between operations  14.5 us (2%)
  starting transfers between devices  9.78 us (1%)
    psum x1, waiting for transfers between devices, shards(): lax.psum(local_grad, ('row', 'col')) * (1.0 / math.sqrt(node_total))  418 us
    reduce_scatter x1, waiting for transfers between devices, shards(): lax.psum_scatter(column_terms.astype(jnp.bfloat16), 'row', scatter_dimens...  101 us
    reduce_scatter x1, waiting for transfers between devices, shards(): lax.psum_scatter(partial_value.astype(jnp.bfloat16), 'col', scatter_dimen...  89.6 us
    all_gather x1, waiting for transfers between devices, shards(): back_slab = lax.all_gather(backward, 'col', axis=0, tiled=True)  65.1 us
    scatter-add x8, other arithmetic, step(): return running.at[target_ids].add(contribution)  35.4 us
    all_to_all x1, waiting for transfers between devices, _solve_things(): lax.all_to_all(jnp.stack([x_local for _ in range(lax.axis_size('row'))],...  25.2 us
  transfers between devices with their start and end apart: 5, of which 5 were waited for; matrix products, arithmetic and copies ran while one was open for 6% of the time, Pallas kernels for 0%

profile of v1, /device:TPU:2, one launch (start us, length us, event | category | flops | bytes accessed | tf_op | source)
XLA Modules:
  0.0 822.5 jit_solution(16018705968732496755)
XLA Ops:
  7.2 2.4 stack.2
  9.6 9.6 %all-to-all-start = ((bf16[32,4096,8]{1,2,0:T(8,128)(2,1)}), bf16[32,4096,8]{1,2,0:T(8,128)(2,1)S(1)}, u32[]{:S(2)}, u32[]{:S(2)}) async-start(bf16[32,4096,8]{1,2,0:T(8,128)(2,1)} %stack.2), calls=%async_computation | async-start | bytes 4194304 | tf_op jit(solution)/shard_map/all_to_all | solution.py:46
  20.0 25.2 %all-to-all-done = bf16[32,4096,8]{1,2,0:T(8,128)(2,1)S(1)} async-done(((bf16[32,4096,8]{1,2,0:T(8,128)(2,1)}), bf16[32,4096,8]{1,2,0:T(8,128)(2,1)S(1)}, u32[]{:S(2)}, u32[]{:S(2)}) %all-to-all-start) | async-done | bytes 2097184 | tf_op jit(solution)/shard_map/all_to_all | solution.py:46
  45.2 1.8 copy.20
  47.0 4.3 copy.16
  52.8 36.0 %while.20 = (s32[]{:T(128)}, f32[16,128,256]{2,1,0:T(8,128)}, s32[]{:T(128)}, s32[96]{0:T(128)S(1)}, s32[]{:T(128)}, /*index=5*/bf16[96,128,128]{2,1,0:T(8,128)(...) while((s32[]{:T(128)}, f32[16,128,256]{2,1,0:T(8,128)}, ...), condition=%wide.region_2.3_spmd, body=%wide.region_0.2_spmd.sunk | while | flops 135791792 | bytes 12063415 | solution.py:39
  53.6 2.2 gather_fusion
  57.4 4.3 scatter_fusion
  62.5 2.2 gather_fusion
  66.3 4.4 scatter_fusion
  71.4 2.2 gather_fusion
  75.3 4.5 scatter_fusion
  80.5 2.2 gather_fusion
  84.3 4.5 scatter_fusion
  88.8 2.8 convert_element_type.24
  91.7 89.6 %reduce-scatter.3.cloned.1.call-done = bf16[128,256]{1,0:T(8,128)(2,1)} async-done(((bf16[2048,256]{1,0:T(8,128)(2,1)}), bf16[128,256]{1,0:T(8,128)(2,1)}) %reduce-scatter.3.cloned.1.call-update) | async-done | bytes 65552 | tf_op jit(solution)/shard_map/reduce_scatter | solution.py:64
  184.0 2.8 copy.14
  187.8 65.1 %all-gather.2.cloned.1.call-done = bf16[2048,256]{1,0:T(8,128)(2,1)} async-done(((bf16[128,256]{1,0:T(8,128)(2,1)}), bf16[2048,256]{1,0:T(8,128)(2,1)}) %all-gather.2.cloned.1.call-update) | async-done | bytes 1048592 | tf_op jit(solution)/shard_map/all_gather | solution.py:75
  252.9 2.4 broadcast_in_dim.59
  255.3 34.6 %while.21 = (s32[]{:T(128)}, f32[32,128,256]{2,1,0:T(8,128)}, s32[]{:T(128)}, s32[96]{0:T(128)S(1)}, s32[]{:T(128)}, /*index=5*/bf16[96,128,128]{1,2,0:T(8,128)(...) while((s32[]{:T(128)}, f32[32,128,256]{2,1,0:T(8,128)}, ...), condition=%wide.region_7.8_spmd, body=%wide.region_5.7_spmd.sunk | while | flops 135791792 | bytes 12063415 | solution.py:39
  256.0 1.8 gather_fusion.1
  259.5 4.3 scatter_fusion.1
  264.6 1.8 gather_fusion.1
  268.1 4.4 scatter_fusion.1
  273.3 1.8 gather_fusion.1
  276.7 4.5 scatter_fusion.1
  282.0 1.8 gather_fusion.1
  285.5 4.5 scatter_fusion.1
  289.9 2.5 convert_element_type.30
  292.4 3.0 copy.19
  295.4 418.3 %all-reduce.2.cloned.1.call-done = f32[256,256]{1,0:T(8,128)} async-done(((f32[256,256]{1,0:T(8,128)}), f32[256,256]{1,0:T(8,128)}) %all-reduce.2.cloned.1.call-update) | async-done | bytes 262160 | tf_op jit(solution)/shard_map/psum | solution.py:73
  715.4 100.6 %reduce-scatter.5.cloned.1.call-done = bf16[4096,8]{0,1:T(8,128)(2,1)} async-done(((bf16[4096,256]{0,1:T(8,128)(2,1)}), bf16[4096,8]{0,1:T(8,128)(2,1)}) %reduce-scatter.5.cloned.1.call-update) | async-done | bytes 65552 | tf_op jit(solution)/shard_map/reduce_scatter | solution.py:81
  (57 shorter events, 25.8 us)
Async XLA Ops:
  7.2 174.2 %copy-start = (bf16[256,256]{1,0:T(8,128)(2,1)S(1)}, bf16[256,256]{1,0:T(8,128)(2,1)}, u32[]{:S(2)}) copy-start(bf16[256,256]{1,0:T(8,128)(2,1)} %param.12) | copy-start | bytes 393220
  9.6 35.6 %all-to-all-start = ((bf16[32,4096,8]{1,2,0:T(8,128)(2,1)}), bf16[32,4096,8]{1,2,0:T(8,128)(2,1)S(1)}, u32[]{:S(2)}, u32[]{:S(2)}) async-start(bf16[32,4096,8]{1,2,0:T(8,128)(2,1)} %stack.2), calls=%async_computation | async-start | bytes 4194304 | tf_op jit(solution)/shard_map/all_to_all | solution.py:46
  19.2 162.1 %reduce-scatter.3.cloned.1.call-start = ((), (), s32[]{:S(2)}) async-start(), calls=%async_computation.3 | async-start | bytes 1114112 | tf_op jit(solution)/shard_map/reduce_scatter | solution.py:64
  51.3 1.5 copy-start.3
  51.3 1.5 copy-start.4
  88.8 92.6 %copy-start.5 = (bf16[128,256]{1,0:T(8,128)(2,1)S(1)}, bf16[128,256]{1,0:T(8,128)(2,1)}, u32[]{:S(2)}) copy-start(bf16[128,256]{1,0:T(8,128)(2,1)} %param.17) | copy-start | bytes 196612
  88.8 95.2 %copy-start.1 = (bf16[96,128,128]{2,1,0:T(8,128)(2,1)S(1)}, bf16[96,128,128]{2,1,0:T(8,128)(2,1)}, u32[]{:S(2)}) copy-start(bf16[96,128,128]{2,1,0:T(8,128)(2,1)} %get-tuple-element.335) | copy-start | bytes 9437188
  91.7 161.2 %all-gather.2.cloned.1.call-start = ((), (), s32[]{:S(2)}) async-start(), calls=%async_computation.5 | async-start | bytes 1114112 | tf_op jit(solution)/shard_map/all_gather | solution.py:75
  183.9 2.9 copy-start.2
  183.9 529.9 %all-reduce.2.cloned.1.call-start = ((), (), s32[]{:S(2)}) async-start(), calls=%async_computation.4 | async-start | bytes 524288 | tf_op jit(solution)/shard_map/psum | solution.py:73
  187.7 628.3 %reduce-scatter.5.cloned.1.call-start = ((), (), s32[]{:S(2)}) async-start(), calls=%async_computation.6 | async-start | bytes 2162688 | tf_op jit(solution)/shard_map/reduce_scatter | solution.py:81
Sparse Core Ops, SparseCore 0:
  91.8 89.5 reduce-scatter.2
  184.2 68.6 all-gather.1
  259.8 453.9 all-reduce.1
  718.6 97.3 reduce-scatter.4
